TPU v7x, 128 devices: a whole 4x4x4 slice. The times are simulated.
128 devices in a mesh: cluster: 8 (over z, core), seq: 16 (over x, y).
Axes of the slice: x: 4, y: 4, z: 4, core: 2. Of those that a mesh axis runs over, the one named last changes fastest.
Arguments:
- nodes: bfloat16 [65536, 1024], P(('cluster', 'seq')), may hold values from -48 to 48
- w_qkv: bfloat16 [1024, 3072], replicated, may hold values from -0.1875 to 0.1875
- w_out: bfloat16 [1024, 1024], replicated, may hold values from -1.5 to 1.5
- kv_ids: int32 [512, 16], P('cluster'), may hold values from 0 to 511, as said below
- counts: int32 [512], P('cluster'), may hold values from 13 to 16, as said below
Outputs:
- attended_out: bfloat16 [65536, 1024], P(('cluster', 'seq'))
Inputs may be any that keep to these rules, and one draw needn't show every extreme that they name: `kv_ids`: entries name blocks; the cluster of block b is b // 64. For query block q, entry 0 is q itself, entries 0 to 11 are distinct blocks of q's cluster, and the last 4 entries are distinct blocks of other clusters. Over all entries of the query blocks of one cluster, at most 16 distinct blocks of any one other cluster are named, and exactly 16 for some pair of clusters. The first counts[q] entries of query block q's list are valid, the others are padding.
All inputs are finite; a program needn't handle non-finite values.
Results may differ from a plain program's by a relative error of at most 0.012.
Values may be sent and summed in bfloat16 or wider, within the bound.
A program may use at most 128 MiB of HBM per device.

v0:
```python
import jax
import jax.numpy as jnp
from jax import lax
from jax.sharding import PartitionSpec as P

D = 1024
HEADS = 16
HD = 64
BLK = 128
KVB = 16
REMOTE = 4


def on_device(nodes, w_qkv, w_out, kv_ids, counts):
    seq_size = lax.axis_size("seq")
    node_rows = nodes.shape[0]
    heads_dev = HEADS // seq_size
    w_grouped = w_qkv.reshape(D, seq_size, heads_dev, 3, HD)
    w_query = w_grouped[:, :, :, 0].reshape(D, seq_size, heads_dev * HD)
    w_keyval = w_grouped[:, :, :, 1:].reshape(D, seq_size, heads_dev * 2 * HD)
    query_proj = jnp.einsum(
        "rd,dsf->srf", nodes, w_query, preferred_element_type=jnp.float32
    ).astype(jnp.bfloat16)
    keyval_proj = jnp.einsum(
        "rd,dsf->srf", nodes, w_keyval, preferred_element_type=jnp.float32
    ).astype(jnp.bfloat16)
    query_recv, keyval_recv = (
        lax.all_to_all(query_proj, "seq", split_axis=0, concat_axis=0, tiled=True),
        lax.all_to_all(keyval_proj, "seq", split_axis=0, concat_axis=0, tiled=True),
    )
    cluster_rows = seq_size * node_rows
    block_count = cluster_rows // BLK
    queries = query_recv.reshape(block_count, BLK, heads_dev, HD)
    keyval_blocks = keyval_recv.reshape(block_count, BLK, heads_dev, 2, HD)
    key_table = jnp.transpose(keyval_blocks[:, :, :, 0], (0, 2, 3, 1))
    value_table = jnp.transpose(keyval_blocks[:, :, :, 1], (0, 2, 1, 3))
    cluster = lax.axis_index("cluster")
    local_ids = kv_ids[:, : KVB - REMOTE] - cluster * block_count
    remote_ids = kv_ids[:, KVB - REMOTE :]
    slot_ids = jnp.arange(KVB, dtype=jnp.int32)
    is_valid = slot_ids[None, :] < counts[:, None]
    far_keys, far_values = (
        lax.all_gather(key_table, "cluster", axis=0, tiled=True),
        lax.all_gather(value_table, "cluster", axis=0, tiled=True),
    )
    groups = block_count // 4
    scale = HD ** (-0.5)

    def attend(packed):
        query_blk, near_ids, far_ids, valid_blk = packed
        near_k = key_table[near_ids]
        far_k = far_keys[far_ids]
        near_v = value_table[near_ids]
        far_v = far_values[far_ids]
        near_scores = (
            jnp.einsum("qahe,qjhek->qhajk", query_blk, near_k, preferred_element_type=jnp.float32)
            * scale
        )
        far_scores = (
            jnp.einsum("qahe,qjhek->qhajk", query_blk, far_k, preferred_element_type=jnp.float32)
            * scale
        )
        near_scores = jnp.where(valid_blk[:, None, None, : KVB - REMOTE, None], near_scores, -1e30)
        far_scores = jnp.where(valid_blk[:, None, None, KVB - REMOTE :, None], far_scores, -1e30)
        row_top = jnp.maximum(
            jnp.max(near_scores, axis=(3, 4), keepdims=True),
            jnp.max(far_scores, axis=(3, 4), keepdims=True),
        )
        near_exp = jnp.exp(near_scores - row_top)
        far_exp = jnp.exp(far_scores - row_top)
        row_total = jnp.sum(near_exp, axis=(3, 4), keepdims=True) + jnp.sum(
            far_exp, axis=(3, 4), keepdims=True
        )
        near_weight = (near_exp / row_total).astype(jnp.bfloat16)
        far_weight = (far_exp / row_total).astype(jnp.bfloat16)
        summed = jnp.einsum(
            "qhajk,qjhke->qahe", near_weight, near_v, preferred_element_type=jnp.float32
        )
        summed = summed + jnp.einsum(
            "qhajk,qjhke->qahe", far_weight, far_v, preferred_element_type=jnp.float32
        )
        return summed.astype(jnp.bfloat16)

    attended = lax.map(
        attend,
        (
            queries.reshape(groups, 4, BLK, heads_dev, HD),
            local_ids.reshape(groups, 4, KVB - REMOTE),
            remote_ids.reshape(groups, 4, REMOTE),
            is_valid.reshape(groups, 4, KVB),
        ),
    )
    attended = attended.reshape(seq_size, node_rows, heads_dev * HD)
    returned = lax.all_to_all(attended, "seq", split_axis=0, concat_axis=0, tiled=True)
    w_split = w_out.reshape(seq_size, heads_dev * HD, D)
    return jnp.einsum("srf,sfd->rd", returned, w_split, preferred_element_type=jnp.float32).astype(
        jnp.bfloat16
    )


def solution(mesh):
    placed = (P(("cluster", "seq"), None), P(), P(), P("cluster", None), P("cluster"))
    return jax.shard_map(
        on_device,
        mesh=mesh,
        in_specs=placed,
        out_specs=P(("cluster", "seq"), None),
        check_vma=False,
    )
```

profile of v0, /device:TPU:0, one launch (start us, length us, event | category | flops | bytes accessed | tf_op | source)
XLA Modules:
  0.0 600.5 jit_solution(15980403184799001119)
XLA Ops:
  6.5 8.8 %copy.22 = bf16[1024,3072]{0,1:T(8,128)(2,1)} copy(bf16[1024,3072]{1,0:T(8,128)(2,1)} %param.8) | data formatting | bytes 12582912 | tf_op args[1]
  15.3 2.7 slice.38
  20.5 35.2 %all_to_all.15 = bf16[16,512,128]{1,2,0:T(8,128)(2,1)S(1)} all-to-all(bf16[16,512,128]{1,2,0:T(8,128)(2,1)S(1)} %convert_bitcast_fusion), channel_id=1, replica_groups=mesh['cluster'=8,'seq'=16] {'seq'}, dimensions={0} | all-to-all | bytes 4194304 | tf_op jit(solution)/shard_map/all_to_all | solution.py:29
  55.7 2.5 copy.23
  58.2 4.4 reshape.168
  62.6 4.0 fusion.18
  67.5 3.9 fusion.14
  71.3 3.9 all-to-all-start.1
  76.2 14.9 %all-to-all-done.1 = bf16[16,512,64]{1,2,0:T(8,128)(2,1)S(1)} async-done(((bf16[16,512,64]{1,2,0:T(8,128)(2,1)}), bf16[16,512,64]{1,2,0:T(8,128)(2,1)S(1)}, u32[]{:S(2)}, u32[]{:S(2)}) %all-to-all-start.1) | async-done | bytes 1048608 | tf_op jit(solution)/shard_map/all_to_all | solution.py:28
  94.3 3.3 copy.26
  97.6 18.4 %all-gather.6.cloned.1.call-done = bf16[512,128,1,1,64]{1,0,4,3,2:T(8,128)(2,1)} async-done(((bf16[64,128,1,1,64]{1,0,4,3,2:T(8,128)(2,1)}), bf16[512,128,1,1,64]{1,0,4,3,2:T(8,128)(2,1)}) %all-gather.6.cloned.1.call-update) | async-done | bytes 8388624 | tf_op jit(solution)/shard_map/all_gather | solution.py:44
  115.9 17.9 %copy.30 = bf16[512,1,128,64]{3,2,1,0:T(8,128)(2,1)} copy(bf16[512,1,128,64]{2,0,3,1:T(8,128)(2,1)} %bitcast.149) | data formatting | bytes 16777216 | tf_op jit(solution)/shard_map/while | solution.py:84
  133.9 33.7 %all-gather.4.cloned.1.call-done = bf16[512,1,64,128]{3,0,2,1:T(8,128)(2,1)} async-done(((bf16[64,1,64,128]{3,0,2,1:T(8,128)(2,1)}), bf16[512,1,64,128]{3,0,2,1:T(8,128)(2,1)}) %all-gather.4.cloned.1.call-update) | async-done | bytes 8388624 | tf_op jit(solution)/shard_map/all_gather | solution.py:43
  167.6 12.0 %copy.29 = bf16[512,1,64,128]{3,2,1,0:T(8,128)(2,1)} copy(bf16[512,1,64,128]{3,0,2,1:T(8,128)(2,1)} %all-gather.4.cloned.1.call-done) | data formatting | bytes 16777216 | tf_op jit(solution)/shard_map/while | solution.py:84
  179.6 386.2 %while.10 = (s32[]{:T(128)}, bf16[16,4,128,1,64]{2,1,4,0,3:T(4,128)(2,1)}, s32[16,4,12]{2,1,0:T(4,128)S(1)}, bf16[64,1,128,64]{3,2,1,0:T(8,128)(2,1)}, pred[16,4...) while((s32[]{:T(128)}, ...), condition=%wide.region_5.6_spmd, body=%wide.region_0.5_spmd.sunk | while | flops 280036544 | bytes 32221496 | solution.py:84
  181.4 4.0 gather_fusion.1
  185.4 7.2 %gather_fusion = bf16[16,128,64]{2,1,0:T(8,128)(2,1)} fusion(bf16[512,128,64]{2,1,0:T(8,128)(2,1)} %bitcast.144, s32[1024]{0:T(1024)S(1)} %pad_clamp_fusion.4), kind=kCustom, calls=%fused_computation.3.clone.1 | custom fusion | bytes 524352 | tf_op jit(solution)/shard_map/while/body/eval_jaxpr/gather | solution.py:54
  194.6 3.6 gather_fusion.3
  205.6 4.0 gather_fusion.1
  209.6 7.2 %gather_fusion = bf16[16,128,64]{2,1,0:T(8,128)(2,1)} fusion(bf16[512,128,64]{2,1,0:T(8,128)(2,1)} %bitcast.144, s32[1024]{0:T(1024)S(1)} %pad_clamp_fusion.4), kind=kCustom, calls=%fused_computation.3.clone.1 | custom fusion | bytes 524352 | tf_op jit(solution)/shard_map/while/body/eval_jaxpr/gather | solution.py:54
  218.7 3.6 gather_fusion.3
  229.7 4.0 gather_fusion.1
  233.7 7.2 %gather_fusion = bf16[16,128,64]{2,1,0:T(8,128)(2,1)} fusion(bf16[512,128,64]{2,1,0:T(8,128)(2,1)} %bitcast.144, s32[1024]{0:T(1024)S(1)} %pad_clamp_fusion.4), kind=kCustom, calls=%fused_computation.3.clone.1 | custom fusion | bytes 524352 | tf_op jit(solution)/shard_map/while/body/eval_jaxpr/gather | solution.py:54
  242.8 3.6 gather_fusion.3
  253.9 4.0 gather_fusion.1
  257.9 7.2 %gather_fusion = bf16[16,128,64]{2,1,0:T(8,128)(2,1)} fusion(bf16[512,128,64]{2,1,0:T(8,128)(2,1)} %bitcast.144, s32[1024]{0:T(1024)S(1)} %pad_clamp_fusion.4), kind=kCustom, calls=%fused_computation.3.clone.1 | custom fusion | bytes 524352 | tf_op jit(solution)/shard_map/while/body/eval_jaxpr/gather | solution.py:54
  267.0 3.6 gather_fusion.3
  278.0 4.0 gather_fusion.1
  282.0 7.2 %gather_fusion = bf16[16,128,64]{2,1,0:T(8,128)(2,1)} fusion(bf16[512,128,64]{2,1,0:T(8,128)(2,1)} %bitcast.144, s32[1024]{0:T(1024)S(1)} %pad_clamp_fusion.4), kind=kCustom, calls=%fused_computation.3.clone.1 | custom fusion | bytes 524352 | tf_op jit(solution)/shard_map/while/body/eval_jaxpr/gather | solution.py:54
  291.1 3.6 gather_fusion.3
  302.1 4.0 gather_fusion.1
  306.1 7.2 %gather_fusion = bf16[16,128,64]{2,1,0:T(8,128)(2,1)} fusion(bf16[512,128,64]{2,1,0:T(8,128)(2,1)} %bitcast.144, s32[1024]{0:T(1024)S(1)} %pad_clamp_fusion.4), kind=kCustom, calls=%fused_computation.3.clone.1 | custom fusion | bytes 524352 | tf_op jit(solution)/shard_map/while/body/eval_jaxpr/gather | solution.py:54
  315.2 3.6 gather_fusion.3
  326.2 4.0 gather_fusion.1
  330.2 7.2 %gather_fusion = bf16[16,128,64]{2,1,0:T(8,128)(2,1)} fusion(bf16[512,128,64]{2,1,0:T(8,128)(2,1)} %bitcast.144, s32[1024]{0:T(1024)S(1)} %pad_clamp_fusion.4), kind=kCustom, calls=%fused_computation.3.clone.1 | custom fusion | bytes 524352 | tf_op jit(solution)/shard_map/while/body/eval_jaxpr/gather | solution.py:54
  339.3 3.6 gather_fusion.3
  350.3 4.0 gather_fusion.1
  354.3 7.2 %gather_fusion = bf16[16,128,64]{2,1,0:T(8,128)(2,1)} fusion(bf16[512,128,64]{2,1,0:T(8,128)(2,1)} %bitcast.144, s32[1024]{0:T(1024)S(1)} %pad_clamp_fusion.4), kind=kCustom, calls=%fused_computation.3.clone.1 | custom fusion | bytes 524352 | tf_op jit(solution)/shard_map/while/body/eval_jaxpr/gather | solution.py:54
  363.4 3.6 gather_fusion.3
  374.5 4.0 gather_fusion.1
  378.5 7.2 %gather_fusion = bf16[16,128,64]{2,1,0:T(8,128)(2,1)} fusion(bf16[512,128,64]{2,1,0:T(8,128)(2,1)} %bitcast.144, s32[1024]{0:T(1024)S(1)} %pad_clamp_fusion.4), kind=kCustom, calls=%fused_computation.3.clone.1 | custom fusion | bytes 524352 | tf_op jit(solution)/shard_map/while/body/eval_jaxpr/gather | solution.py:54
  387.6 3.6 gather_fusion.3
  398.7 4.0 gather_fusion.1
  402.7 7.2 %gather_fusion = bf16[16,128,64]{2,1,0:T(8,128)(2,1)} fusion(bf16[512,128,64]{2,1,0:T(8,128)(2,1)} %bitcast.144, s32[1024]{0:T(1024)S(1)} %pad_clamp_fusion.4), kind=kCustom, calls=%fused_computation.3.clone.1 | custom fusion | bytes 524352 | tf_op jit(solution)/shard_map/while/body/eval_jaxpr/gather | solution.py:54
  411.8 3.6 gather_fusion.3
  422.8 4.0 gather_fusion.1
  426.8 7.2 %gather_fusion = bf16[16,128,64]{2,1,0:T(8,128)(2,1)} fusion(bf16[512,128,64]{2,1,0:T(8,128)(2,1)} %bitcast.144, s32[1024]{0:T(1024)S(1)} %pad_clamp_fusion.4), kind=kCustom, calls=%fused_computation.3.clone.1 | custom fusion | bytes 524352 | tf_op jit(solution)/shard_map/while/body/eval_jaxpr/gather | solution.py:54
  435.9 3.6 gather_fusion.3
  447.0 4.0 gather_fusion.1
  451.0 7.2 %gather_fusion = bf16[16,128,64]{2,1,0:T(8,128)(2,1)} fusion(bf16[512,128,64]{2,1,0:T(8,128)(2,1)} %bitcast.144, s32[1024]{0:T(1024)S(1)} %pad_clamp_fusion.4), kind=kCustom, calls=%fused_computation.3.clone.1 | custom fusion | bytes 524352 | tf_op jit(solution)/shard_map/while/body/eval_jaxpr/gather | solution.py:54
  460.1 3.6 gather_fusion.3
  471.1 4.0 gather_fusion.1
  475.1 7.2 %gather_fusion = bf16[16,128,64]{2,1,0:T(8,128)(2,1)} fusion(bf16[512,128,64]{2,1,0:T(8,128)(2,1)} %bitcast.144, s32[1024]{0:T(1024)S(1)} %pad_clamp_fusion.4), kind=kCustom, calls=%fused_computation.3.clone.1 | custom fusion | bytes 524352 | tf_op jit(solution)/shard_map/while/body/eval_jaxpr/gather | solution.py:54
  484.2 3.6 gather_fusion.3
  495.2 4.0 gather_fusion.1
  499.2 7.2 %gather_fusion = bf16[16,128,64]{2,1,0:T(8,128)(2,1)} fusion(bf16[512,128,64]{2,1,0:T(8,128)(2,1)} %bitcast.144, s32[1024]{0:T(1024)S(1)} %pad_clamp_fusion.4), kind=kCustom, calls=%fused_computation.3.clone.1 | custom fusion | bytes 524352 | tf_op jit(solution)/shard_map/while/body/eval_jaxpr/gather | solution.py:54
  508.3 3.6 gather_fusion.3
  519.4 4.0 gather_fusion.1
  523.4 7.2 %gather_fusion = bf16[16,128,64]{2,1,0:T(8,128)(2,1)} fusion(bf16[512,128,64]{2,1,0:T(8,128)(2,1)} %bitcast.144, s32[1024]{0:T(1024)S(1)} %pad_clamp_fusion.4), kind=kCustom, calls=%fused_computation.3.clone.1 | custom fusion | bytes 524352 | tf_op jit(solution)/shard_map/while/body/eval_jaxpr/gather | solution.py:54
  532.5 3.6 gather_fusion.3
  543.5 4.0 gather_fusion.1
  547.5 7.2 %gather_fusion = bf16[16,128,64]{2,1,0:T(8,128)(2,1)} fusion(bf16[512,128,64]{2,1,0:T(8,128)(2,1)} %bitcast.144, s32[1024]{0:T(1024)S(1)} %pad_clamp_fusion.4), kind=kCustom, calls=%fused_computation.3.clone.1 | custom fusion | bytes 524352 | tf_op jit(solution)/shard_map/while/body/eval_jaxpr/gather | solution.py:54
  556.6 3.6 gather_fusion.3
  567.3 24.1 %all_to_all.16 = bf16[16,512,64]{1,2,0:T(8,128)(2,1)S(1)} all-to-all(bf16[16,512,64]{1,2,0:T(8,128)(2,1)S(1)} %reshape.170), channel_id=1, replica_groups=mesh['cluster'=8,'seq'=16] {'seq'}, dimensions={0} | all-to-all | bytes 2097152 | tf_op jit(solution)/shard_map/all_to_all | solution.py:94
  (456 shorter events, 160.2 us)
Async XLA Ops:
  6.5 584.9 %copy-start = (bf16[1024,1024]{1,0:T(8,128)(2,1)S(1)}, bf16[1024,1024]{1,0:T(8,128)(2,1)}, u32[]{:S(2)}) copy-start(bf16[1024,1024]{1,0:T(8,128)(2,1)} %param.9) | copy-start | bytes 6291460
  6.5 109.4 %all-gather.6.cloned.1.call-start = ((), (), s32[]{:S(2)}) async-start(), calls=%async_computation.4 | async-start | bytes 9437184 | tf_op jit(solution)/shard_map/all_gather | solution.py:44
  15.3 2.7 copy-start.7
  66.7 100.9 %all-gather.4.cloned.1.call-start = ((), (), s32[]{:S(2)}) async-start(), calls=%async_computation.3 | async-start | bytes 9437184 | tf_op jit(solution)/shard_map/all_gather | solution.py:43
  67.4 7.8 %copy-start.5 = (s32[64,16]{0,1:T(8,128)S(1)}, s32[64,16]{0,1:T(8,128)}, u32[]{:S(2)}) copy-start(s32[64,16]{0,1:T(8,128)} %param.10) | copy-start | bytes 12292
  67.4 7.8 %copy-start.6 = (s32[64]{0:T(128)S(1)}, s32[64]{0:T(128)}, u32[]{:S(2)}) copy-start(s32[64]{0:T(128)} %param.11) | copy-start | bytes 772
  71.3 19.8 %all-to-all-start.1 = ((bf16[16,512,64]{1,2,0:T(8,128)(2,1)}), bf16[16,512,64]{1,2,0:T(8,128)(2,1)S(1)}, u32[]{:S(2)}, u32[]{:S(2)}) async-start(bf16[16,512,64]{1,2,0:T(8,128)(2,1)} %fusion.14), calls=%async_computation.1 | async-start | bytes 2097152 | tf_op jit(solution)/shard_map/all_to_all | solution.py:28
  179.6 14.5 %copy-start.2 = (bf16[64,1,64,128]{3,2,1,0:T(8,128)(2,1)}, bf16[64,1,64,128]{3,2,1,0:T(8,128)(2,1)S(1)}, u32[]{:S(2)}) copy-start(bf16[64,1,64,128]{3,2,1,0:T(8,128)(2,1)S(1)} %get-tuple-element.202) | copy-start | bytes 3145732 | tf_op jit(solution)/shard_map/while
  198.2 3.2 copy-start.4
  200.5 1.4 copy-start.1
  201.9 1.9 copy-start.3
  203.8 14.5 %copy-start.2 = (bf16[64,1,64,128]{3,2,1,0:T(8,128)(2,1)}, bf16[64,1,64,128]{3,2,1,0:T(8,128)(2,1)S(1)}, u32[]{:S(2)}) copy-start(bf16[64,1,64,128]{3,2,1,0:T(8,128)(2,1)S(1)} %get-tuple-element.202) | copy-start | bytes 3145732 | tf_op jit(solution)/shard_map/while
  222.3 3.2 copy-start.4
  224.6 1.4 copy-start.1
  226.0 1.9 copy-start.3
  227.9 14.5 %copy-start.2 = (bf16[64,1,64,128]{3,2,1,0:T(8,128)(2,1)}, bf16[64,1,64,128]{3,2,1,0:T(8,128)(2,1)S(1)}, u32[]{:S(2)}) copy-start(bf16[64,1,64,128]{3,2,1,0:T(8,128)(2,1)S(1)} %get-tuple-element.202) | copy-start | bytes 3145732 | tf_op jit(solution)/shard_map/while
  246.4 3.2 copy-start.4
  248.8 1.4 copy-start.1
  250.2 1.9 copy-start.3
  252.1 14.6 %copy-start.2 = (bf16[64,1,64,128]{3,2,1,0:T(8,128)(2,1)}, bf16[64,1,64,128]{3,2,1,0:T(8,128)(2,1)S(1)}, u32[]{:S(2)}) copy-start(bf16[64,1,64,128]{3,2,1,0:T(8,128)(2,1)S(1)} %get-tuple-element.202) | copy-start | bytes 3145732 | tf_op jit(solution)/shard_map/while
  270.6 3.2 copy-start.4
  272.9 1.4 copy-start.1
  274.3 1.9 copy-start.3
  276.2 14.5 %copy-start.2 = (bf16[64,1,64,128]{3,2,1,0:T(8,128)(2,1)}, bf16[64,1,64,128]{3,2,1,0:T(8,128)(2,1)S(1)}, u32[]{:S(2)}) copy-start(bf16[64,1,64,128]{3,2,1,0:T(8,128)(2,1)S(1)} %get-tuple-element.202) | copy-start | bytes 3145732 | tf_op jit(solution)/shard_map/while
  294.7 3.2 copy-start.4
  297.0 1.4 copy-start.1
  298.5 1.9 copy-start.3
  300.4 14.5 %copy-start.2 = (bf16[64,1,64,128]{3,2,1,0:T(8,128)(2,1)}, bf16[64,1,64,128]{3,2,1,0:T(8,128)(2,1)S(1)}, u32[]{:S(2)}) copy-start(bf16[64,1,64,128]{3,2,1,0:T(8,128)(2,1)S(1)} %get-tuple-element.202) | copy-start | bytes 3145732 | tf_op jit(solution)/shard_map/while
  318.8 3.2 copy-start.4
  321.1 1.4 copy-start.1
  322.6 1.9 copy-start.3
  324.5 14.5 %copy-start.2 = (bf16[64,1,64,128]{3,2,1,0:T(8,128)(2,1)}, bf16[64,1,64,128]{3,2,1,0:T(8,128)(2,1)S(1)}, u32[]{:S(2)}) copy-start(bf16[64,1,64,128]{3,2,1,0:T(8,128)(2,1)S(1)} %get-tuple-element.202) | copy-start | bytes 3145732 | tf_op jit(solution)/shard_map/while
  342.9 3.2 copy-start.4
  345.2 1.4 copy-start.1
  346.7 1.9 copy-start.3
  348.6 14.5 %copy-start.2 = (bf16[64,1,64,128]{3,2,1,0:T(8,128)(2,1)}, bf16[64,1,64,128]{3,2,1,0:T(8,128)(2,1)S(1)}, u32[]{:S(2)}) copy-start(bf16[64,1,64,128]{3,2,1,0:T(8,128)(2,1)S(1)} %get-tuple-element.202) | copy-start | bytes 3145732 | tf_op jit(solution)/shard_map/while
  367.0 3.2 copy-start.4
  369.3 1.4 copy-start.1
  370.8 1.9 copy-start.3
  372.7 14.6 %copy-start.2 = (bf16[64,1,64,128]{3,2,1,0:T(8,128)(2,1)}, bf16[64,1,64,128]{3,2,1,0:T(8,128)(2,1)S(1)}, u32[]{:S(2)}) copy-start(bf16[64,1,64,128]{3,2,1,0:T(8,128)(2,1)S(1)} %get-tuple-element.202) | copy-start | bytes 3145732 | tf_op jit(solution)/shard_map/while
  391.2 3.2 copy-start.4
  393.5 1.4 copy-start.1
  394.9 1.9 copy-start.3
  396.8 14.6 %copy-start.2 = (bf16[64,1,64,128]{3,2,1,0:T(8,128)(2,1)}, bf16[64,1,64,128]{3,2,1,0:T(8,128)(2,1)S(1)}, u32[]{:S(2)}) copy-start(bf16[64,1,64,128]{3,2,1,0:T(8,128)(2,1)S(1)} %get-tuple-element.202) | copy-start | bytes 3145732 | tf_op jit(solution)/shard_map/while
  415.4 3.2 copy-start.4
  419.1 1.9 copy-start.3
  421.0 14.5 %copy-start.2 = (bf16[64,1,64,128]{3,2,1,0:T(8,128)(2,1)}, bf16[64,1,64,128]{3,2,1,0:T(8,128)(2,1)S(1)}, u32[]{:S(2)}) copy-start(bf16[64,1,64,128]{3,2,1,0:T(8,128)(2,1)S(1)} %get-tuple-element.202) | copy-start | bytes 3145732 | tf_op jit(solution)/shard_map/while
  439.5 3.2 copy-start.4
  443.3 1.9 copy-start.3
  445.2 14.5 %copy-start.2 = (bf16[64,1,64,128]{3,2,1,0:T(8,128)(2,1)}, bf16[64,1,64,128]{3,2,1,0:T(8,128)(2,1)S(1)}, u32[]{:S(2)}) copy-start(bf16[64,1,64,128]{3,2,1,0:T(8,128)(2,1)S(1)} %get-tuple-element.202) | copy-start | bytes 3145732 | tf_op jit(solution)/shard_map/while
  463.7 3.2 copy-start.4
  467.4 1.9 copy-start.3
  469.3 14.5 %copy-start.2 = (bf16[64,1,64,128]{3,2,1,0:T(8,128)(2,1)}, bf16[64,1,64,128]{3,2,1,0:T(8,128)(2,1)S(1)}, u32[]{:S(2)}) copy-start(bf16[64,1,64,128]{3,2,1,0:T(8,128)(2,1)S(1)} %get-tuple-element.202) | copy-start | bytes 3145732 | tf_op jit(solution)/shard_map/while
  487.8 3.2 copy-start.4
  491.5 1.9 copy-start.3
  493.4 14.5 %copy-start.2 = (bf16[64,1,64,128]{3,2,1,0:T(8,128)(2,1)}, bf16[64,1,64,128]{3,2,1,0:T(8,128)(2,1)S(1)}, u32[]{:S(2)}) copy-start(bf16[64,1,64,128]{3,2,1,0:T(8,128)(2,1)S(1)} %get-tuple-element.202) | copy-start | bytes 3145732 | tf_op jit(solution)/shard_map/while
  511.9 3.2 copy-start.4
  515.7 1.9 copy-start.3
  517.6 14.5 %copy-start.2 = (bf16[64,1,64,128]{3,2,1,0:T(8,128)(2,1)}, bf16[64,1,64,128]{3,2,1,0:T(8,128)(2,1)S(1)}, u32[]{:S(2)}) copy-start(bf16[64,1,64,128]{3,2,1,0:T(8,128)(2,1)S(1)} %get-tuple-element.202) | copy-start | bytes 3145732 | tf_op jit(solution)/shard_map/while
  536.1 3.2 copy-start.4
  539.8 1.9 copy-start.3
  541.7 14.5 %copy-start.2 = (bf16[64,1,64,128]{3,2,1,0:T(8,128)(2,1)}, bf16[64,1,64,128]{3,2,1,0:T(8,128)(2,1)S(1)}, u32[]{:S(2)}) copy-start(bf16[64,1,64,128]{3,2,1,0:T(8,128)(2,1)S(1)} %get-tuple-element.202) | copy-start | bytes 3145732 | tf_op jit(solution)/shard_map/while
  560.2 3.2 copy-start.4
  563.9 1.9 copy-start.3
  (7 other events, 9.9 us)
Sparse Core Ops, SparseCore 0:
  66.8 49.0 all-gather.5
  117.6 49.9 all-gather.3
where the time goes:
time: 605 us; the launch traced here: 601 us
  local copies, waits for them, and re-layouts  364 us (60%)
  matrix products  74.1 us (12%)
  waiting for transfers between devices  67.7 us (11%)
  blocking collectives  59.3 us (10%)
  other arithmetic  16.9 us (3%)
  between operations  13.5 us (2%)
    gather x16, local copies, waits for them, and re-layouts, attend(): far_v = far_values[far_ids]  115 us
    gather x16, local copies, waits for them, and re-layouts, attend(): far_k = far_keys[far_ids]  63.7 us
    gather x16, local copies, waits for them, and re-layouts, attend(): near_v = value_table[near_ids]  57.6 us
    while x4, local copies, waits for them, and re-layouts, on_device(): lax.map(attend, (queries.reshape(groups, 4, BLK, heads_dev, HD), local_id...  35.3 us
    all_to_all x1, blocking collectives, on_device(): lax.all_to_all(keyval_proj, 'seq', split_axis=0, concat_axis=0, tiled=True)  35.2 us
    dot_general x16, matrix products, attend(): jnp.einsum('qahe,qjhek->qhajk', query_blk, near_k, preferred_element_type...  34.2 us
    all_gather x1, waiting for transfers between devices, on_device(): lax.all_gather(key_table, 'cluster', axis=0, tiled=True)  33.7 us
    gather x16, local copies, waits for them, and re-layouts, attend(): near_k = key_table[near_ids]  24.9 us
  transfers between devices with their start and end apart: 3, of which 3 were waited for; matrix products, arithmetic and copies ran while one was open for 5% of the time, Pallas kernels for 0%

commit v1 on v0

--- a/solution.py
+++ b/solution.py
@@ -40,7 +40,10 @@
     slot_ids = jnp.arange(KVB, dtype=jnp.int32)
     is_valid = slot_ids[None, :] < counts[:, None]
     far_keys, far_values = (
-        lax.all_gather(key_table, "cluster", axis=0, tiled=True),
+        jnp.concatenate(
+            lax.all_to_all(jnp.stack([key_table] * lax.axis_size("cluster")), "cluster", 0, 0),
+            axis=0,
+        ),
         lax.all_gather(value_table, "cluster", axis=0, tiled=True),
     )
     groups = block_count // 4

time: 605 us -> 629 us (1.040)
  waiting for transfers between devices: 67.7 us -> 90.5 us
    all_to_all x0 -> x1, waiting for transfers between devices: none -> 54.1 us  [on_device(): lax.all_to_all(jnp.stack([key_table] * lax.axis_size('cluster')), 'cluste...]
    all_gather x1 -> x0, waiting for transfers between devices: 33.7 us -> none  [on_device(): lax.all_gather(key_table, 'cluster', axis=0, tiled=True)]
    while x4 -> x3, local copies, waits for them, and re-layouts: 35.3 us -> 22.9 us  [on_device(): lax.map(attend, (queries.reshape(groups, 4, BLK, heads_dev, HD), local_id...]
  transfers between devices with their start and end apart: 3 -> 3, of which waited for: 3 -> 3; matrix products, arithmetic and copies ran while one was open for 5% -> 6% of each run, Pallas kernels for 0% -> 0%
where the time goes in v1:
time: 629 us; the launch traced here: 625 us
  local copies, waits for them, and re-layouts  360 us (57%)
  waiting for transfers between devices  90.5 us (14%)
  matrix products  74.1 us (12%)
  blocking collectives  58.7 us (9%)
  other arithmetic  16.9 us (3%)
  between operations  13.5 us (2%)
  starting transfers between devices  9.78 us (2%)
    gather x16, local copies, waits for them, and re-layouts, attend(): far_v = far_values[far_ids]  115 us
    gather x16, local copies, waits for them, and re-layouts, attend(): far_k = far_keys[far_ids]  63.7 us
    gather x16, local copies, waits for them, and re-layouts, attend(): near_v = value_table[near_ids]  57.7 us
    all_to_all x1, waiting for transfers between devices, on_device(): lax.all_to_all(jnp.stack([key_table] * lax.axis_size('cluster')), 'cluste...  54.1 us
    all_to_all x1, blocking collectives, on_device(): lax.all_to_all(keyval_proj, 'seq', split_axis=0, concat_axis=0, tiled=True)  35.2 us
    dot_general x16, matrix products, attend(): jnp.einsum('qahe,qjhek->qhajk', query_blk, near_k, preferred_element_type...  34.2 us
    gather x16, local copies, waits for them, and re-layouts, attend(): near_k = key_table[near_ids]  24.9 us
    all_to_all x1, blocking collectives, on_device(): lax.all_to_all(attended, 'seq', split_axis=0, concat_axis=0, tiled=True)  23.5 us
  transfers between devices with their start and end apart: 3, of which 3 were waited for; matrix products, arithmetic and copies ran while one was open for 6% of the time, Pallas kernels for 0%

profile of v1, /device:TPU:0, one launch (start us, length us, event | category | flops | bytes accessed | tf_op | source)
XLA Modules:
  0.0 624.6 jit_solution(9404751591347741222)
XLA Ops:
  6.5 8.8 %copy.37 = bf16[1024,3072]{0,1:T(8,128)(2,1)} copy(bf16[1024,3072]{1,0:T(8,128)(2,1)} %param.8) | data formatting | bytes 12582912 | tf_op args[1]
  15.3 2.7 slice.38
  20.5 35.2 %all_to_all.20 = bf16[16,512,128]{1,2,0:T(8,128)(2,1)S(1)} all-to-all(bf16[16,512,128]{1,2,0:T(8,128)(2,1)S(1)} %convert_bitcast_fusion), channel_id=1, replica_groups=mesh['cluster'=8,'seq'=16] {'seq'}, dimensions={0} | all-to-all | bytes 4194304 | tf_op jit(solution)/shard_map/all_to_all | solution.py:29
  58.2 4.4 reshape.174
  62.6 4.4 fusion.18
  67.0 3.9 fusion.14
  70.9 4.3 all-to-all-start.1
  77.2 13.6 %all-to-all-done.1 = bf16[16,512,64]{1,2,0:T(8,128)(2,1)} async-done(((bf16[16,512,64]{1,2,0:T(8,128)(2,1)}), bf16[16,512,64]{1,2,0:T(8,128)(2,1)}, u32[]{:S(2)}, u32[]{:S(2)}) %all-to-all-start.1) | async-done | bytes 1048608 | tf_op jit(solution)/shard_map/all_to_all | solution.py:28
  90.8 5.4 stack.2
  96.2 5.4 all-to-all-start.2
  106.7 3.4 copy.42
  110.1 22.9 %all-gather.3.cloned.1.call-done = bf16[512,128,1,1,64]{1,0,4,3,2:T(8,128)(2,1)} async-done(((bf16[64,128,1,1,64]{1,0,4,3,2:T(8,128)(2,1)}), bf16[512,128,1,1,64]{1,0,4,3,2:T(8,128)(2,1)}) %all-gather.3.cloned.1.call-update) | async-done | bytes 8388624 | tf_op jit(solution)/shard_map/all_gather | solution.py:47
  133.0 17.6 %copy.46 = bf16[512,1,128,64]{3,2,1,0:T(8,128)(2,1)} copy(bf16[512,1,128,64]{2,0,3,1:T(8,128)(2,1)} %bitcast.154) | data formatting | bytes 16777216 | tf_op jit(solution)/shard_map/while | solution.py:87
  150.6 54.1 %all-to-all-done.2 = bf16[8,64,1,64,128]{4,3,1,2,0:T(8,128)(2,1)} async-done(((bf16[8,64,1,64,128]{4,3,1,2,0:T(8,128)(2,1)}), bf16[8,64,1,64,128]{4,3,1,2,0:T(8,128)(2,1)}, u32[]{:S(2)}, u32[]{:S(2)}) %all-to-all-start.2) | async-done | bytes 8388640 | tf_op jit(solution)/shard_map/all_to_all | solution.py:44
  204.7 385.8 %while.10 = (s32[]{:T(128)}, bf16[16,4,128,1,64]{2,1,4,0,3:T(4,128)(2,1)}, s32[16,4,12]{2,1,0:T(4,128)S(1)}, bf16[64,1,128,64]{3,2,1,0:T(8,128)(2,1)}, pred[16,4...) while((s32[]{:T(128)}, ...), condition=%wide.region_5.6_spmd, body=%wide.region_0.5_spmd.sunk | while | flops 280036544 | bytes 32221496 | solution.py:87
  206.5 4.0 gather_fusion.1
  210.4 7.2 %gather_fusion = bf16[16,128,64]{2,1,0:T(8,128)(2,1)} fusion(bf16[512,128,64]{2,1,0:T(8,128)(2,1)} %bitcast.150, s32[1024]{0:T(1024)S(1)} %pad_clamp_fusion.4), kind=kCustom, calls=%fused_computation.3.clone.1 | custom fusion | bytes 524352 | tf_op jit(solution)/shard_map/while/body/eval_jaxpr/gather | solution.py:57
  219.6 3.6 gather_fusion.3
  230.6 4.0 gather_fusion.1
  234.6 7.2 %gather_fusion = bf16[16,128,64]{2,1,0:T(8,128)(2,1)} fusion(bf16[512,128,64]{2,1,0:T(8,128)(2,1)} %bitcast.150, s32[1024]{0:T(1024)S(1)} %pad_clamp_fusion.4), kind=kCustom, calls=%fused_computation.3.clone.1 | custom fusion | bytes 524352 | tf_op jit(solution)/shard_map/while/body/eval_jaxpr/gather | solution.py:57
  243.7 3.6 gather_fusion.3
  254.7 4.0 gather_fusion.1
  258.6 7.2 %gather_fusion = bf16[16,128,64]{2,1,0:T(8,128)(2,1)} fusion(bf16[512,128,64]{2,1,0:T(8,128)(2,1)} %bitcast.150, s32[1024]{0:T(1024)S(1)} %pad_clamp_fusion.4), kind=kCustom, calls=%fused_computation.3.clone.1 | custom fusion | bytes 524352 | tf_op jit(solution)/shard_map/while/body/eval_jaxpr/gather | solution.py:57
  267.8 3.6 gather_fusion.3
  278.8 4.0 gather_fusion.1
  282.8 7.2 %gather_fusion = bf16[16,128,64]{2,1,0:T(8,128)(2,1)} fusion(bf16[512,128,64]{2,1,0:T(8,128)(2,1)} %bitcast.150, s32[1024]{0:T(1024)S(1)} %pad_clamp_fusion.4), kind=kCustom, calls=%fused_computation.3.clone.1 | custom fusion | bytes 524352 | tf_op jit(solution)/shard_map/while/body/eval_jaxpr/gather | solution.py:57
  291.9 3.6 gather_fusion.3
  302.8 4.0 gather_fusion.1
  306.8 7.2 %gather_fusion = bf16[16,128,64]{2,1,0:T(8,128)(2,1)} fusion(bf16[512,128,64]{2,1,0:T(8,128)(2,1)} %bitcast.150, s32[1024]{0:T(1024)S(1)} %pad_clamp_fusion.4), kind=kCustom, calls=%fused_computation.3.clone.1 | custom fusion | bytes 524352 | tf_op jit(solution)/shard_map/while/body/eval_jaxpr/gather | solution.py:57
  315.9 3.6 gather_fusion.3
  327.0 4.0 gather_fusion.1
  331.0 7.2 %gather_fusion = bf16[16,128,64]{2,1,0:T(8,128)(2,1)} fusion(bf16[512,128,64]{2,1,0:T(8,128)(2,1)} %bitcast.150, s32[1024]{0:T(1024)S(1)} %pad_clamp_fusion.4), kind=kCustom, calls=%fused_computation.3.clone.1 | custom fusion | bytes 524352 | tf_op jit(solution)/shard_map/while/body/eval_jaxpr/gather | solution.py:57
  340.1 3.6 gather_fusion.3
  351.1 4.0 gather_fusion.1
  355.1 7.2 %gather_fusion = bf16[16,128,64]{2,1,0:T(8,128)(2,1)} fusion(bf16[512,128,64]{2,1,0:T(8,128)(2,1)} %bitcast.150, s32[1024]{0:T(1024)S(1)} %pad_clamp_fusion.4), kind=kCustom, calls=%fused_computation.3.clone.1 | custom fusion | bytes 524352 | tf_op jit(solution)/shard_map/while/body/eval_jaxpr/gather | solution.py:57
  364.2 3.6 gather_fusion.3
  375.2 4.0 gather_fusion.1
  379.2 7.2 %gather_fusion = bf16[16,128,64]{2,1,0:T(8,128)(2,1)} fusion(bf16[512,128,64]{2,1,0:T(8,128)(2,1)} %bitcast.150, s32[1024]{0:T(1024)S(1)} %pad_clamp_fusion.4), kind=kCustom, calls=%fused_computation.3.clone.1 | custom fusion | bytes 524352 | tf_op jit(solution)/shard_map/while/body/eval_jaxpr/gather | solution.py:57
  388.3 3.6 gather_fusion.3
  399.3 4.0 gather_fusion.1
  403.3 7.2 %gather_fusion = bf16[16,128,64]{2,1,0:T(8,128)(2,1)} fusion(bf16[512,128,64]{2,1,0:T(8,128)(2,1)} %bitcast.150, s32[1024]{0:T(1024)S(1)} %pad_clamp_fusion.4), kind=kCustom, calls=%fused_computation.3.clone.1 | custom fusion | bytes 524352 | tf_op jit(solution)/shard_map/while/body/eval_jaxpr/gather | solution.py:57
  412.4 3.6 gather_fusion.3
  423.5 4.0 gather_fusion.1
  427.5 7.2 %gather_fusion = bf16[16,128,64]{2,1,0:T(8,128)(2,1)} fusion(bf16[512,128,64]{2,1,0:T(8,128)(2,1)} %bitcast.150, s32[1024]{0:T(1024)S(1)} %pad_clamp_fusion.4), kind=kCustom, calls=%fused_computation.3.clone.1 | custom fusion | bytes 524352 | tf_op jit(solution)/shard_map/while/body/eval_jaxpr/gather | solution.py:57
  436.6 3.6 gather_fusion.3
  447.6 4.0 gather_fusion.1
  451.6 7.2 %gather_fusion = bf16[16,128,64]{2,1,0:T(8,128)(2,1)} fusion(bf16[512,128,64]{2,1,0:T(8,128)(2,1)} %bitcast.150, s32[1024]{0:T(1024)S(1)} %pad_clamp_fusion.4), kind=kCustom, calls=%fused_computation.3.clone.1 | custom fusion | bytes 524352 | tf_op jit(solution)/shard_map/while/body/eval_jaxpr/gather | solution.py:57
  460.8 3.6 gather_fusion.3
  471.8 4.0 gather_fusion.1
  475.7 7.2 %gather_fusion = bf16[16,128,64]{2,1,0:T(8,128)(2,1)} fusion(bf16[512,128,64]{2,1,0:T(8,128)(2,1)} %bitcast.150, s32[1024]{0:T(1024)S(1)} %pad_clamp_fusion.4), kind=kCustom, calls=%fused_computation.3.clone.1 | custom fusion | bytes 524352 | tf_op jit(solution)/shard_map/while/body/eval_jaxpr/gather | solution.py:57
  484.9 3.6 gather_fusion.3
  495.8 4.0 gather_fusion.1
  499.8 7.2 %gather_fusion = bf16[16,128,64]{2,1,0:T(8,128)(2,1)} fusion(bf16[512,128,64]{2,1,0:T(8,128)(2,1)} %bitcast.150, s32[1024]{0:T(1024)S(1)} %pad_clamp_fusion.4), kind=kCustom, calls=%fused_computation.3.clone.1 | custom fusion | bytes 524352 | tf_op jit(solution)/shard_map/while/body/eval_jaxpr/gather | solution.py:57
  508.9 3.6 gather_fusion.3
  519.9 4.0 gather_fusion.1
  523.9 7.2 %gather_fusion = bf16[16,128,64]{2,1,0:T(8,128)(2,1)} fusion(bf16[512,128,64]{2,1,0:T(8,128)(2,1)} %bitcast.150, s32[1024]{0:T(1024)S(1)} %pad_clamp_fusion.4), kind=kCustom, calls=%fused_computation.3.clone.1 | custom fusion | bytes 524352 | tf_op jit(solution)/shard_map/while/body/eval_jaxpr/gather | solution.py:57
  533.0 3.6 gather_fusion.3
  544.0 4.0 gather_fusion.1
  548.0 7.2 %gather_fusion = bf16[16,128,64]{2,1,0:T(8,128)(2,1)} fusion(bf16[512,128,64]{2,1,0:T(8,128)(2,1)} %bitcast.150, s32[1024]{0:T(1024)S(1)} %pad_clamp_fusion.4), kind=kCustom, calls=%fused_computation.3.clone.1 | custom fusion | bytes 524352 | tf_op jit(solution)/shard_map/while/body/eval_jaxpr/gather | solution.py:57
  557.1 3.6 gather_fusion.3
  568.1 4.0 gather_fusion.1
  572.1 7.2 %gather_fusion = bf16[16,128,64]{2,1,0:T(8,128)(2,1)} fusion(bf16[512,128,64]{2,1,0:T(8,128)(2,1)} %bitcast.150, s32[1024]{0:T(1024)S(1)} %pad_clamp_fusion.4), kind=kCustom, calls=%fused_computation.3.clone.1 | custom fusion | bytes 524352 | tf_op jit(solution)/shard_map/while/body/eval_jaxpr/gather | solution.py:57
  581.2 3.6 gather_fusion.3
  591.9 23.5 %all_to_all.21 = bf16[16,512,64]{1,2,0:T(8,128)(2,1)S(1)} all-to-all(bf16[16,512,64]{1,2,0:T(8,128)(2,1)S(1)} %reshape.177), channel_id=1, replica_groups=mesh['cluster'=8,'seq'=16] {'seq'}, dimensions={0} | all-to-all | bytes 2097152 | tf_op jit(solution)/shard_map/all_to_all | solution.py:97
  (456 shorter events, 164.8 us)
Async XLA Ops:
  6.5 608.9 %copy-start = (bf16[1024,1024]{1,0:T(8,128)(2,1)S(1)}, bf16[1024,1024]{1,0:T(8,128)(2,1)}, u32[]{:S(2)}) copy-start(bf16[1024,1024]{1,0:T(8,128)(2,1)} %param.9) | copy-start | bytes 6291460
  6.5 126.4 %all-gather.3.cloned.1.call-start = ((), (), s32[]{:S(2)}) async-start(), calls=%async_computation.4 | async-start | bytes 9437184 | tf_op jit(solution)/shard_map/all_gather | solution.py:47
  15.3 2.7 copy-start.7
  70.9 19.9 %all-to-all-start.1 = ((bf16[16,512,64]{1,2,0:T(8,128)(2,1)}), bf16[16,512,64]{1,2,0:T(8,128)(2,1)}, u32[]{:S(2)}, u32[]{:S(2)}) async-start(bf16[16,512,64]{1,2,0:T(8,128)(2,1)} %fusion.14), calls=%async_computation.1 | async-start | bytes 2097152 | tf_op jit(solution)/shard_map/all_to_all | solution.py:28
  96.2 5.5 copy-start.5
  96.2 5.5 copy-start.6
  96.2 108.5 %all-to-all-start.2 = ((bf16[8,64,1,64,128]{4,3,1,2,0:T(8,128)(2,1)}), bf16[8,64,1,64,128]{4,3,1,2,0:T(8,128)(2,1)}, u32[]{:S(2)}, u32[]{:S(2)}) async-start(bf16[8,64,1,64,128]{4,3,1,2,0:T(8,128)(2,1)} %stack.2), calls=%async_computation.2 | async-start | bytes 16777216 | tf_op jit(solution)/shard_map/all_to_all | solution.py:44
  204.7 14.5 %copy-start.2 = (bf16[64,1,64,128]{3,2,1,0:T(8,128)(2,1)}, bf16[64,1,64,128]{3,2,1,0:T(8,128)(2,1)S(1)}, u32[]{:S(2)}) copy-start(bf16[64,1,64,128]{3,2,1,0:T(8,128)(2,1)S(1)} %get-tuple-element.213) | copy-start | bytes 3145732 | tf_op jit(solution)/shard_map/while
  223.2 3.2 copy-start.4
  225.5 1.4 copy-start.1
  226.9 1.9 copy-start.3
  228.8 14.5 %copy-start.2 = (bf16[64,1,64,128]{3,2,1,0:T(8,128)(2,1)}, bf16[64,1,64,128]{3,2,1,0:T(8,128)(2,1)S(1)}, u32[]{:S(2)}) copy-start(bf16[64,1,64,128]{3,2,1,0:T(8,128)(2,1)S(1)} %get-tuple-element.213) | copy-start | bytes 3145732 | tf_op jit(solution)/shard_map/while
  247.3 3.2 copy-start.4
  249.6 1.4 copy-start.1
  251.0 1.9 copy-start.3
  252.9 14.5 %copy-start.2 = (bf16[64,1,64,128]{3,2,1,0:T(8,128)(2,1)}, bf16[64,1,64,128]{3,2,1,0:T(8,128)(2,1)S(1)}, u32[]{:S(2)}) copy-start(bf16[64,1,64,128]{3,2,1,0:T(8,128)(2,1)S(1)} %get-tuple-element.213) | copy-start | bytes 3145732 | tf_op jit(solution)/shard_map/while
  271.4 3.2 copy-start.4
  273.7 1.4 copy-start.1
  275.1 1.9 copy-start.3
  277.0 14.5 %copy-start.2 = (bf16[64,1,64,128]{3,2,1,0:T(8,128)(2,1)}, bf16[64,1,64,128]{3,2,1,0:T(8,128)(2,1)S(1)}, u32[]{:S(2)}) copy-start(bf16[64,1,64,128]{3,2,1,0:T(8,128)(2,1)S(1)} %get-tuple-element.213) | copy-start | bytes 3145732 | tf_op jit(solution)/shard_map/while
  295.5 3.2 copy-start.4
  297.8 1.4 copy-start.1
  299.2 1.9 copy-start.3
  301.1 14.4 %copy-start.2 = (bf16[64,1,64,128]{3,2,1,0:T(8,128)(2,1)}, bf16[64,1,64,128]{3,2,1,0:T(8,128)(2,1)S(1)}, u32[]{:S(2)}) copy-start(bf16[64,1,64,128]{3,2,1,0:T(8,128)(2,1)S(1)} %get-tuple-element.213) | copy-start | bytes 3145732 | tf_op jit(solution)/shard_map/while
  319.5 3.2 copy-start.4
  321.9 1.4 copy-start.1
  323.3 1.9 copy-start.3
  325.2 14.5 %copy-start.2 = (bf16[64,1,64,128]{3,2,1,0:T(8,128)(2,1)}, bf16[64,1,64,128]{3,2,1,0:T(8,128)(2,1)S(1)}, u32[]{:S(2)}) copy-start(bf16[64,1,64,128]{3,2,1,0:T(8,128)(2,1)S(1)} %get-tuple-element.213) | copy-start | bytes 3145732 | tf_op jit(solution)/shard_map/while
  343.7 3.2 copy-start.4
  346.0 1.4 copy-start.1
  347.4 1.9 copy-start.3
  349.3 14.5 %copy-start.2 = (bf16[64,1,64,128]{3,2,1,0:T(8,128)(2,1)}, bf16[64,1,64,128]{3,2,1,0:T(8,128)(2,1)S(1)}, u32[]{:S(2)}) copy-start(bf16[64,1,64,128]{3,2,1,0:T(8,128)(2,1)S(1)} %get-tuple-element.213) | copy-start | bytes 3145732 | tf_op jit(solution)/shard_map/while
  367.9 3.2 copy-start.4
  370.2 1.4 copy-start.1
  371.6 1.9 copy-start.3
  373.5 14.5 %copy-start.2 = (bf16[64,1,64,128]{3,2,1,0:T(8,128)(2,1)}, bf16[64,1,64,128]{3,2,1,0:T(8,128)(2,1)S(1)}, u32[]{:S(2)}) copy-start(bf16[64,1,64,128]{3,2,1,0:T(8,128)(2,1)S(1)} %get-tuple-element.213) | copy-start | bytes 3145732 | tf_op jit(solution)/shard_map/while
  391.9 3.2 copy-start.4
  394.3 1.4 copy-start.1
  395.7 1.9 copy-start.3
  397.6 14.5 %copy-start.2 = (bf16[64,1,64,128]{3,2,1,0:T(8,128)(2,1)}, bf16[64,1,64,128]{3,2,1,0:T(8,128)(2,1)S(1)}, u32[]{:S(2)}) copy-start(bf16[64,1,64,128]{3,2,1,0:T(8,128)(2,1)S(1)} %get-tuple-element.213) | copy-start | bytes 3145732 | tf_op jit(solution)/shard_map/while
  416.0 3.2 copy-start.4
  418.4 1.4 copy-start.1
  419.8 1.9 copy-start.3
  421.7 14.5 %copy-start.2 = (bf16[64,1,64,128]{3,2,1,0:T(8,128)(2,1)}, bf16[64,1,64,128]{3,2,1,0:T(8,128)(2,1)S(1)}, u32[]{:S(2)}) copy-start(bf16[64,1,64,128]{3,2,1,0:T(8,128)(2,1)S(1)} %get-tuple-element.213) | copy-start | bytes 3145732 | tf_op jit(solution)/shard_map/while
  440.2 3.2 copy-start.4
  443.9 1.9 copy-start.3
  445.8 14.5 %copy-start.2 = (bf16[64,1,64,128]{3,2,1,0:T(8,128)(2,1)}, bf16[64,1,64,128]{3,2,1,0:T(8,128)(2,1)S(1)}, u32[]{:S(2)}) copy-start(bf16[64,1,64,128]{3,2,1,0:T(8,128)(2,1)S(1)} %get-tuple-element.213) | copy-start | bytes 3145732 | tf_op jit(solution)/shard_map/while
  464.4 3.2 copy-start.4
  468.1 1.9 copy-start.3
  470.0 14.5 %copy-start.2 = (bf16[64,1,64,128]{3,2,1,0:T(8,128)(2,1)}, bf16[64,1,64,128]{3,2,1,0:T(8,128)(2,1)S(1)}, u32[]{:S(2)}) copy-start(bf16[64,1,64,128]{3,2,1,0:T(8,128)(2,1)S(1)} %get-tuple-element.213) | copy-start | bytes 3145732 | tf_op jit(solution)/shard_map/while
  488.5 3.2 copy-start.4
  492.2 1.9 copy-start.3
  494.1 14.4 %copy-start.2 = (bf16[64,1,64,128]{3,2,1,0:T(8,128)(2,1)}, bf16[64,1,64,128]{3,2,1,0:T(8,128)(2,1)S(1)}, u32[]{:S(2)}) copy-start(bf16[64,1,64,128]{3,2,1,0:T(8,128)(2,1)S(1)} %get-tuple-element.213) | copy-start | bytes 3145732 | tf_op jit(solution)/shard_map/while
  512.5 3.2 copy-start.4
  516.3 1.9 copy-start.3
  518.2 14.5 %copy-start.2 = (bf16[64,1,64,128]{3,2,1,0:T(8,128)(2,1)}, bf16[64,1,64,128]{3,2,1,0:T(8,128)(2,1)S(1)}, u32[]{:S(2)}) copy-start(bf16[64,1,64,128]{3,2,1,0:T(8,128)(2,1)S(1)} %get-tuple-element.213) | copy-start | bytes 3145732 | tf_op jit(solution)/shard_map/while
  536.6 3.2 copy-start.4
  540.3 1.9 copy-start.3
  542.2 14.4 %copy-start.2 = (bf16[64,1,64,128]{3,2,1,0:T(8,128)(2,1)}, bf16[64,1,64,128]{3,2,1,0:T(8,128)(2,1)S(1)}, u32[]{:S(2)}) copy-start(bf16[64,1,64,128]{3,2,1,0:T(8,128)(2,1)S(1)} %get-tuple-element.213) | copy-start | bytes 3145732 | tf_op jit(solution)/shard_map/while
  560.7 3.2 copy-start.4
  564.4 1.9 copy-start.3
  566.3 14.5 %copy-start.2 = (bf16[64,1,64,128]{3,2,1,0:T(8,128)(2,1)}, bf16[64,1,64,128]{3,2,1,0:T(8,128)(2,1)S(1)}, u32[]{:S(2)}) copy-start(bf16[64,1,64,128]{3,2,1,0:T(8,128)(2,1)S(1)} %get-tuple-element.213) | copy-start | bytes 3145732 | tf_op jit(solution)/shard_map/while
  584.8 3.2 copy-start.4
  588.6 1.9 copy-start.3
  (7 other events, 9.9 us)
Sparse Core Ops, SparseCore 0:
  67.1 65.7 all-gather.2
